TPU v7x, 32 devices: a whole 2x2x4 slice. The times are simulated.
32 devices in a mesh: seq: 8 (over z, y), batch: 4 (over x, core).
Axes of the slice: x: 2, y: 2, z: 4, core: 2. Of those that a mesh axis runs over, the one named last changes fastest.
Arguments:
- queries: bfloat16 [8192, 256], P(('batch', 'seq')), parts along dimension 0, may hold values from -0.5 to 0.5
- keys: bfloat16 [8192, 256], P(('batch', 'seq')), parts along dimension 0, may hold values from -0.5 to 0.5
- values: bfloat16 [8192, 512], P(('batch', 'seq')), parts along dimension 0, may hold values from -6 to 6
- log_decay: float32 [8192, 256], P(('batch', 'seq')), parts along dimension 0, may hold values from -1 to 0, as said below
- out_grad: bfloat16 [8192, 512], P(('batch', 'seq')), parts along dimension 0, may hold values from -0.19921875 to 0.19921875
Outputs:
- grad_queries: bfloat16 [8192, 256], P(('batch', 'seq')), parts along dimension 0
- grad_keys: bfloat16 [8192, 256], P(('batch', 'seq')), parts along dimension 0
- grad_values: bfloat16 [8192, 512], P(('batch', 'seq')), parts along dimension 0
- grad_decay: float32 [8192, 256], P(('batch', 'seq')), parts along dimension 0
There are 4 independent parts, one for each index of `batch`. A program takes and returns all parts, laid end to end along the dimension named above; each array names one. Nothing has to cross between parts.
Inputs may be any that keep to these rules, and one draw needn't show every extreme that they name: `log_decay`: log of a decay factor per position and key channel.
All inputs are finite; a program needn't handle non-finite values.
Results may differ from a plain program's by a relative error of at most 0.001.
Values sent between devices are 32-bit elements; how exact they have to be, the bound alone decides.
A program may use at most 128 MiB of HBM per device.

v0:
```python
import jax
import jax.numpy as jnp
from jax import lax
from jax.sharding import PartitionSpec as P

H = 2
K = 128
V = 256
GROUP = 64


HIGHEST_PRECISION = lax.Precision.HIGHEST


def carried_in(part, axis, combine, identity, reverse):
    count = lax.axis_size(axis)
    place = lax.axis_index(axis)
    ahead = count - 1 - place if reverse else place
    gathered = jax.tree.map(lambda a: lax.all_gather(a, axis), part)
    state = jax.tree.map(lambda a, e: jnp.zeros_like(a) + jnp.asarray(e, a.dtype), part, identity)

    def one(turn, state):
        source = count - 1 - turn if reverse else turn
        return combine(
            state, jax.tree.map(lambda a: lax.dynamic_index_in_dim(a, source, 0, False), gathered)
        )

    return lax.fori_loop(0, ahead, one, state)


def outer_product(form, left, right):
    return jnp.einsum(
        form, left, right, precision=HIGHEST_PRECISION, preferred_element_type=jnp.float32
    )


def pair_combine(earlier, later_one):
    return (earlier[0] + later_one[0], jnp.exp(later_one[0])[..., None] * earlier[1] + later_one[1])


def joined_combine(earlier, later_one):
    summed_decay = earlier[0] + later_one[0]
    grad_state = jnp.exp(later_one[0])[..., None] * earlier[1] + later_one[1]
    weight = earlier[2] + jnp.exp(earlier[0])[..., None] * later_one[2]
    counted = earlier[3] + later_one[3] - jnp.sum(earlier[1] * later_one[2], axis=-1)
    return (summed_decay, grad_state, weight, counted)


def local(queries, keys, values, log_decay, out_grad):
    input_symbols = queries.shape[0]
    blocks = input_symbols // GROUP
    query_rows = queries.reshape(blocks, GROUP, H, K).astype(jnp.float32)
    key_rows = keys.reshape(blocks, GROUP, H, K).astype(jnp.float32)
    value_bf = values.reshape(blocks, GROUP, H, V)
    grad_bf = out_grad.reshape(blocks, GROUP, H, V)
    value_rows = value_bf.astype(jnp.float32)
    grad_rows = grad_bf.astype(jnp.float32)
    within = jnp.cumsum(log_decay.reshape(blocks, GROUP, H, K), axis=1)
    block_sum = within[:, -1]
    rising = jnp.exp(within)
    falling = jnp.exp(-within)
    tail_gate = jnp.exp(block_sum[:, None] - within)
    q_gate = query_rows * rising
    k_gate = key_rows * falling
    k_tail = key_rows * tail_gate
    local_ends = outer_product("nchk,nchv->nhkv", k_tail, value_rows)
    local_starts = outer_product("nchk,nchv->nhkv", q_gate, grad_rows)
    zero_state = jnp.zeros((H, K, V), jnp.float32)
    zero_decay = jnp.zeros((H, K), jnp.float32)

    def forward_step(carried_state, inputs):
        summed_decay, end_state = inputs
        return (jnp.exp(summed_decay)[..., None] * carried_state + end_state, carried_state)

    device_end, prefix = lax.scan(forward_step, zero_state, (block_sum, local_ends))

    def backward_step(carried_gradient, inputs):
        summed_decay, start_grad = inputs
        return (start_grad + jnp.exp(summed_decay)[..., None] * carried_gradient, carried_gradient)

    device_start, suffix = lax.scan(
        backward_step, zero_state, (block_sum, local_starts), reverse=True
    )
    device_total = jnp.sum(block_sum, axis=0)
    through = lax.cumsum(block_sum, axis=0)
    prior_decay = through - block_sum
    after_decay = device_total[None] - through
    entry_pair = carried_in(
        (device_total, device_end), "seq", pair_combine, (zero_decay, zero_state), False
    )
    starts = prefix + jnp.exp(prior_decay)[..., None] * entry_pair[1]
    causal = jnp.tril(jnp.ones((GROUP, GROUP), jnp.float32))
    score_matrix = outer_product("nthk,nshk->nhts", q_gate, k_gate) * causal
    pair_dots = (
        jnp.einsum("nthv,nshv->nhts", grad_bf, value_bf, preferred_element_type=jnp.float32)
        * causal
    )
    grad_q = rising * (
        outer_product("nhts,nshk->nthk", pair_dots, k_gate)
        + outer_product("nthv,nhkv->nthk", grad_rows, starts)
    )
    inner_k = falling * outer_product("nhts,nthk->nshk", pair_dots, q_gate)
    local_sum = jnp.sum(query_rows * grad_q - key_rows * inner_k, axis=(0, 1)) - jnp.sum(
        suffix * local_ends, axis=(0, 3)
    )
    joined = carried_in(
        (device_total, device_start, device_end, local_sum),
        "seq",
        joined_combine,
        (zero_decay, zero_state, zero_state, zero_decay),
        True,
    )
    exit_grad = joined[1]
    later_sum = joined[3].reshape(H * K)
    grads_in = suffix + jnp.exp(after_decay)[..., None] * exit_grad
    grad_k = inner_k + tail_gate * outer_product("nshv,nhkv->nshk", value_rows, grads_in)
    value_gradient = outer_product("nhts,nthv->nshv", score_matrix, grad_rows) + outer_product(
        "nshk,nhkv->nshv", k_tail, grads_in
    )
    dg_terms = (query_rows * grad_q - key_rows * grad_k).reshape(input_symbols, H * K)
    running = lax.cumsum(dg_terms, axis=0, reverse=True)
    grad_decay = running + later_sum[None, :]
    return (
        grad_q.reshape(input_symbols, H * K).astype(jnp.bfloat16),
        grad_k.reshape(input_symbols, H * K).astype(jnp.bfloat16),
        value_gradient.reshape(input_symbols, H * V).astype(jnp.bfloat16),
        grad_decay,
    )


def solution(mesh):
    return jax.shard_map(
        local,
        mesh=mesh,
        in_specs=(
            P(("batch", "seq"), None),
            P(("batch", "seq"), None),
            P(("batch", "seq"), None),
            P(("batch", "seq"), None),
            P(("batch", "seq"), None),
        ),
        out_specs=(
            P(("batch", "seq"), None),
            P(("batch", "seq"), None),
            P(("batch", "seq"), None),
            P(("batch", "seq"), None),
        ),
        check_vma=False,
    )
```

profile of v0, /device:TPU:0, one launch (start us, length us, event | category | flops | bytes accessed | tf_op | source)
XLA Modules:
  0.0 153.8 jit_solution(6281938518831663048)
XLA Ops:
  7.2 0.0 all-gather.9.cloned.1.call-start
  7.2 1.0 reshape.117
  8.3 1.1 reshape.111
  9.4 0.1 fusion.41
  9.5 1.0 reshape.112
  10.5 1.0 reshape.118
  11.5 1.6 %fusion.33 = f32[4,2,128,256]{3,2,1,0:T(8,128)} fusion(bf16[4,64,2,256]{3,2,1,0:T(2,128)(2,1)S(1)} %reshape.112, f32[4,64,2,128]{3,2,1,0:T(2,128)S(1)} %reshape.118, f32[4,64,2,128]{3,2,1,0:T(2,128)S(1)} %fusion.41), kind=kOutput, calls=%fused_computation.60 | convolution fusion | flops 201392128 | bytes 1835008 | tf_op jit(solution)/shard_map/nchk,nchv->nhkv/dot_general | solution.py:32
  13.1 0.1 broadcast.23.clone
  13.2 0.0 copy-start.7
  13.2 4.6 %while.62 = (s32[]{:T(128)}, f32[2,128,256]{2,1,0:T(8,128)S(1)}, f32[4,2,128,256]{3,2,1,0:T(8,128)S(1)}, f32[4,2,128,256]{3,2,1,0:T(8,128)}, f32[4,2,128]{2,1,0:T(2,128)S(1)}, /*index=5*/s32[]{:T(128)}, s32[]{:T(128)}, s32[]{:T(128)}) while((s32[]{:T(128)}, f32[2,128,256]{2,1,0:T(8,128)S(1)}, f32[4,2,128,256]{3,2,1,0:T(8,128)S(1)}, ...), condition=%wide.region_8.9_spmd.clone, body=%wide.region_7.8_spmd.clone.sunk | while | flops 262148 | bytes 1313920 | solution.py:81
  13.3 1.1 bitcast_add_fusion.11
  14.5 1.1 bitcast_add_fusion.11
  15.6 1.1 bitcast_add_fusion.11
  16.8 1.1 bitcast_add_fusion.11
  17.8 0.0 copy-done.7
  17.9 0.0 copy-start.1
  17.9 0.1 reshape.113
  17.9 1.6 %multiply_reduce_fusion = (f32[2,128]{1,0:T(2,128)S(1)}, f32[4,2,128,256]{3,2,1,0:T(8,128)}) fusion(f32[4,2,128,256]{3,2,1,0:T(8,128)S(1)} %get-tuple-element.314, bf16[4,64,2,256]{3,2,1,0:T(2,128)(2,1)S(1)} %reshape.113, f32[4,64,2,128]{3,2,1,0:T(2,128)S(1)} %reshape.117, f32[4,64,2,128]{3,2,1,0:T(2,128)S(1)} %fusion.41, ...), kind=kOutput, calls=%fused_computation.29 | convolution fusion | flops 201981696 | bytes 2888704 | tf_op jit(solution)/shard_map/nchk,nchv->nhkv/dot_general | solution.py:32
  19.6 1.1 broadcast.23
  20.6 0.0 copy-done.1
  20.6 7.3 %while.61 = (s32[]{:T(128)}, f32[2,128,256]{2,1,0:T(8,128)S(1)}, f32[4,2,128,256]{3,2,1,0:T(8,128)}, f32[4,2,128]{2,1,0:T(2,128)S(1)}, f32[4,2,128,256]{3,2,1,0:T(8,128)}, /*index=5*/s32[]{:T(128)}, s32[]{:T(128)}) while((s32[]{:T(128)}, f32[2,128,256]{2,1,0:T(8,128)S(1)}, f32[4,2,128,256]{3,2,1,0:T(8,128)}, ...), condition=%wide.region_2.3_spmd.clone, body=%wide.region_1.2_spmd.clone.sunk | while | flops 262147 | bytes 1313900 | solution.py:75
  20.6 0.7 bitcast_dynamic-update-slice_fusion.4
  21.4 1.1 bitcast_add_fusion.10
  22.4 0.7 bitcast_dynamic-update-slice_fusion.4
  23.2 1.1 bitcast_add_fusion.10
  24.3 0.7 bitcast_dynamic-update-slice_fusion.4
  25.0 1.1 bitcast_add_fusion.10
  26.1 0.7 bitcast_dynamic-update-slice_fusion.4
  26.8 1.1 bitcast_add_fusion.10
  27.9 0.0 copy-start
  27.9 0.7 copy-done
  28.6 0.0 all-gather.9.cloned.1.call-update
  28.6 0.0 all-gather.11.cloned.1.call-start
  28.7 0.7 all-gather.11.cloned.1.call-update
  29.4 22.4 %all-gather.4 = f32[8,2,128]{2,1,0:T(2,128)S(1)} all-gather(f32[1,2,128]{2,1,0:T(2,128)S(1)} %bitcast.129), channel_id=2, replica_groups=mesh['seq'=8,'batch'=4] {'seq'}, dimensions={0}, use_global_device_ids=true | all-gather | bytes 9216 | tf_op jit(solution)/shard_map/all_gather | solution.py:19
  51.9 0.9 convolution_multiply_fusion.1
  52.8 0.6 convolution_multiply_fusion
  53.4 1.2 convolution_bitcast_fusion.1
  54.6 26.2 %all-gather.9.cloned.1.call-done = f32[16,128,256]{2,1,0:T(8,128)} async-done(((f32[2,128,256]{2,1,0:T(8,128)}), f32[16,128,256]{2,1,0:T(8,128)}) %all-gather.9.cloned.1.call-update) | async-done | bytes 2097168 | tf_op jit(solution)/shard_map/all_gather | solution.py:19
  80.8 0.0 copy-start.5
  80.8 1.2 copy-done.2
  82.0 0.9 fusion.9
  82.9 1.4 fusion.6
  84.3 0.6 subtract_reduce_fusion
  84.9 24.8 %all-gather.5 = f32[8,2,128]{2,1,0:T(2,128)S(1)} all-gather(f32[1,2,128]{2,1,0:T(2,128)S(1)} %subtract_bitcast_fusion), channel_id=5, replica_groups=mesh['seq'=8,'batch'=4] {'seq'}, dimensions={0}, use_global_device_ids=true | all-gather | bytes 9216 | tf_op jit(solution)/shard_map/all_gather | solution.py:19
  109.7 21.1 %all-gather.11.cloned.1.call-done = f32[16,128,256]{2,1,0:T(8,128)} async-done(((f32[2,128,256]{2,1,0:T(8,128)}), f32[16,128,256]{2,1,0:T(8,128)}) %all-gather.11.cloned.1.call-update) | async-done | bytes 2097168 | tf_op jit(solution)/shard_map/all_gather | solution.py:19
  130.9 8.9 %while.60 = (s32[]{:T(128)}, f32[2,128,256]{2,1,0:T(8,128)S(1)}, f32[2,128]{1,0:T(2,128)S(1)}, s32[]{:T(128)}, f32[8,2,128]{2,1,0:T(2,128)S(1)}, /*index=5*/f32[...) while((s32[]{:T(128)}, f32[2,128,256]{2,1,0:T(8,128)S(1)}, ...), condition=%wide.region_13.14_spmd, body=%wide.region_11.13_spmd.sunk | while | flops 262406 | bytes 1056951 | solution.py:28
  130.9 1.2 fusion.48
  132.2 1.2 fusion.48
  133.5 1.2 fusion.48
  134.7 1.2 fusion.48
  136.0 1.2 fusion.48
  137.3 1.2 fusion.48
  138.5 1.2 fusion.48
  139.8 0.9 multiply_subtract_fusion
  140.7 0.1 copy.61
  140.8 0.1 copy.54
  141.0 0.9 fusion.3
  141.9 0.3 copy.64
  142.2 0.7 copy.73
  142.9 0.2 copy.66
  143.1 2.3 %fusion.18 = f32[256,2,128]{0,1,2:T(2,128)S(1)} fusion(f32[256,2,128]{0,2,1:T(8,128)S(1)} %bitcast.121), kind=kOutput, calls=%fused_computation.41 | output fusion | flops 8323072 | bytes 524288 | tf_op jit(solution)/shard_map/reduce-window
  145.5 0.7 copy_bitcast_fusion.1
  146.3 0.7 bitcast_add_fusion.5
  (51 shorter events, 0.6 us)
Async XLA Ops:
  7.2 73.6 %all-gather.9.cloned.1.call-start = ((), (), s32[]{:S(2)}) async-start(), calls=%async_computation | async-start | bytes 2359296 | tf_op jit(solution)/shard_map/all_gather | solution.py:19
  13.2 4.6 %copy-start.7 = (bf16[256,512]{1,0:T(8,128)(2,1)S(1)}, bf16[256,512]{1,0:T(8,128)(2,1)}, u32[]{:S(2)}) copy-start(bf16[256,512]{1,0:T(8,128)(2,1)} %param.15) | copy-start | bytes 786436
  17.9 2.8 %copy-start.1 = (f32[2,128,256]{2,1,0:T(8,128)}, f32[2,128,256]{2,1,0:T(8,128)S(1)}, u32[]{:S(2)}) copy-start(f32[2,128,256]{2,1,0:T(8,128)S(1)} %get-tuple-element.315) | copy-start | bytes 786436
  17.9 33.9 %copy-start.3 = (bf16[4,64,2,256]{3,2,1,0:T(2,128)(2,1)}, bf16[4,64,2,256]{3,2,1,0:T(2,128)(2,1)S(1)}, u32[]{:S(2)}) copy-start(bf16[4,64,2,256]{3,2,1,0:T(2,128)(2,1)S(1)} %reshape.113) | copy-start | bytes 786436
  27.9 0.7 copy-start
  28.6 102.2 %all-gather.11.cloned.1.call-start = ((), (), s32[]{:S(2)}) async-start(), calls=%async_computation.1 | async-start | bytes 2359296 | tf_op jit(solution)/shard_map/all_gather | solution.py:19
  80.8 1.2 copy-start.2
  80.8 3.4 %copy-start.5 = (f32[4,2,64,64]{3,2,1,0:T(8,128)S(1)}, f32[4,2,64,64]{3,2,1,0:T(8,128)}, u32[]{:S(2)}) copy-start(f32[4,2,64,64]{3,2,1,0:T(8,128)} %convolution_multiply_fusion.1) | copy-start | bytes 393220
  130.9 8.9 %copy-start.4 = (bf16[4,64,2,256]{3,2,1,0:T(2,128)(2,1)S(1)}, bf16[4,64,2,256]{3,2,1,0:T(2,128)(2,1)}, u32[]{:S(2)}) copy-start(bf16[4,64,2,256]{3,2,1,0:T(2,128)(2,1)} %copy-done.3) | copy-start | bytes 786436
  139.8 1.2 copy-start.6
Sparse Core Ops, SparseCore 0:
  28.8 51.9 all-gather.8
  82.9 47.8 all-gather.10
where the time goes:
time: 154 us
  waiting for transfers between devices  48 us (31%)
  blocking collectives  47.3 us (31%)
  other arithmetic  23.3 us (15%)
  between operations  14.3 us (9%)
  matrix products  10.6 us (7%)
  local copies, waits for them, and re-layouts  9.71 us (6%)
    all_gather x2, waiting for transfers between devices, carried_in(): gathered = jax.tree.map(lambda a: lax.all_gather(a, axis), part)  47.3 us
    all_gather x2, blocking collectives, carried_in(): gathered = jax.tree.map(lambda a: lax.all_gather(a, axis), part)  47.3 us
    dot_general x9, matrix products, outer_product(): jnp.einsum(form, left, right, precision=HIGHEST_PRECISION, preferred_elem...  9.71 us
    reduce_sum x7, other arithmetic, joined_combine(): jnp.sum(earlier[1] * later_one[2], axis=-1)  8.44 us
    add x4, other arithmetic, backward_step(): start_grad + jnp.exp(summed_decay)[..., None] * carried_gradient  4.28 us
    add x4, other arithmetic, forward_step(): jnp.exp(summed_decay)[..., None] * carried_state + end_state  4.28 us
  transfers between devices with their start and end apart: 2, of which 2 were waited for; matrix products, arithmetic and copies ran while one was open for 4% of the time, Pallas kernels for 0%

commit v1 on v0

v1 whole, which is shorter than its diff:
```python
import functools

import jax
import jax.numpy as jnp
from jax import lax
from jax.experimental import pallas as pl
from jax.experimental.pallas import tpu as pltpu
from jax.sharding import PartitionSpec as P

H = 2
GROUP = 64
ROWS = 64

F32 = jnp.float32
BF16 = jnp.bfloat16


def split(x):
    hi = x.astype(BF16)
    return hi, (x - hi.astype(F32)).astype(BF16)


def mm(a, b):
    return lax.dot_general(a, b, (((1,), (0,)), ((), ())), preferred_element_type=F32)


def mm_nt(a, b):
    return lax.dot_general(a, b, (((1,), (1,)), ((), ())), preferred_element_type=F32)


def mm_tn(a, b):
    return lax.dot_general(a, b, (((0,), (0,)), ((), ())), preferred_element_type=F32)


def three(dot, a, b):
    return dot(a[0], b[0]) + dot(a[0], b[1]) + dot(a[1], b[0])


def kernel(n_seq, L, K, V,
           q_hbm, k_hbm, v_hbm, ld_hbm, do_hbm,
           dq_hbm, dk_hbm, dv_hbm, gd_hbm,
           q_ref, k_ref, v_ref, ld_ref, do_ref,
           dq_ref, dk_ref, dv_ref, gd_ref,
           acc_q, acc_k, acc_v, rise_ref, tail_ref, whole_rise, whole_tail, kt_ref, qg_ref,
           loc, px, carry, total, ent, ec_own, ec_par,
           in_sem, out_sem, ec_sem, px_send, px_recv, near_send, near_recv, far_send, far_recv):
    blocks = L // GROUP
    per_head = V // ROWS
    chunks = H * per_head
    me = lax.axis_index("seq")
    odd = lax.rem(me, 2)
    mine = 1 - odd
    other = odd
    sign = 2 * odd - 1
    partner = me - sign
    near = me + sign
    far = me + 2 * sign
    back = me - 2 * sign
    has_dst = jnp.logical_and(far >= 0, far < n_seq)
    has_src = jnp.logical_and(back >= 0, back < n_seq)
    peers = 1 + 2 * has_dst.astype(jnp.int32) + has_src.astype(jnp.int32)
    barrier = pltpu.get_barrier_semaphore()

    loads = [
        pltpu.make_async_copy(src, dst, in_sem.at[i])
        for i, (src, dst) in enumerate(
            ((ld_hbm, ld_ref), (k_hbm, k_ref), (v_hbm, v_ref), (q_hbm, q_ref), (do_hbm, do_ref))
        )
    ]
    for copy in loads:
        copy.start()

    def tell(device):
        pl.semaphore_signal(barrier, inc=1, device_id={"seq": device},
                            device_id_type=pl.DeviceIdType.MESH)

    tell(partner)

    @pl.when(has_dst)
    def _():
        tell(near)
        tell(far)

    @pl.when(has_src)
    def _():
        tell(back)

    loads[0].wait()
    row = lax.broadcasted_iota(jnp.int32, (L, L), 0)
    col = lax.broadcasted_iota(jnp.int32, (L, L), 1)
    within = jnp.logical_and(row >= col, row // GROUP == col // GROUP)
    tri = jnp.where(within, 1.0, 0.0).astype(BF16)
    ld = ld_ref[...]
    ld0, rest = split(ld)
    mid = ld - ld0.astype(F32)
    low = (mid - rest.astype(F32)).astype(BF16)
    b = mm(tri, ld0) + mm(tri, rest) + mm(tri, low)

    def rows(n):
        return slice(n * GROUP, (n + 1) * GROUP)

    def cols(h):
        return slice(h * K, (h + 1) * K)

    def vcols(h):
        return slice(h * V, (h + 1) * V)

    c = [b[(n + 1) * GROUP - 1:(n + 1) * GROUP, :] for n in range(blocks)]
    before = [jnp.zeros_like(c[0])]
    for n in range(blocks):
        before.append(before[-1] + c[n])
    after = [jnp.zeros_like(c[0])]
    for n in reversed(range(blocks)):
        after.insert(0, after[0] + c[n])
    for n in range(blocks):
        bn = b[rows(n), :]
        rise = jnp.exp(bn)
        tail = jnp.exp(c[n] - bn)
        rise_ref[rows(n), :] = rise
        tail_ref[rows(n), :] = tail
        whole_rise[rows(n), :] = rise * jnp.exp(before[n])
        whole_tail[rows(n), :] = tail * jnp.exp(after[n + 1])
    gone = jnp.exp(before[blocks])
    for h in range(H):
        ec_own[h] = jnp.broadcast_to(gone[:, cols(h)], (8, K))

    def send(src, dst, ssem, rsem, device):
        return pltpu.make_async_remote_copy(
            src_ref=src, dst_ref=dst, send_sem=ssem, recv_sem=rsem,
            device_id={"seq": device}, device_id_type=pl.DeviceIdType.MESH)

    def part(i):
        return i // per_head, pl.ds((i % per_head) * ROWS, ROWS)

    def px_copy(i):
        h, r = part(i)
        return send(loc.at[other, h, r], px.at[h, r], px_send.at[i], px_recv.at[i], partner)

    def near_copy(i):
        h, r = part(i)
        return send(total.at[h, r], ent.at[mine, h, r], near_send.at[i], near_recv.at[i], near)

    def far_copy(i):
        h, r = part(i)
        return send(total.at[h, r], carry.at[h, r], far_send.at[i], far_recv.at[i], far)

    ec_copy = send(ec_own, ec_par, ec_sem.at[0], ec_sem.at[1], partner)

    for copy in loads[1:]:
        copy.wait()
    for h in range(H):
        ke = split(k_ref[:, cols(h)].astype(F32) * whole_tail[:, cols(h)])
        kt_ref[0, :, cols(h)] = ke[0]
        kt_ref[1, :, cols(h)] = ke[1]
        e = mm_tn(v_ref[:, vcols(h)], jnp.concatenate(ke, axis=1))
        loc[0, h] = e[:, :K] + e[:, K:]
        qf = split(q_ref[:, cols(h)].astype(F32) * whole_rise[:, cols(h)])
        f = mm_tn(do_ref[:, vcols(h)], jnp.concatenate(qf, axis=1))
        loc[1, h] = f[:, :K] + f[:, K:]
        if h == 0:
            pl.semaphore_wait(barrier, peers)
            ec_copy.start()
        for i in range(h * per_head, (h + 1) * per_head):
            px_copy(i).start()

    for h in range(H):
        k = k_ref[:, cols(h)].astype(F32)
        q = q_ref[:, cols(h)].astype(F32)
        v = v_ref[:, vcols(h)]
        do = do_ref[:, vcols(h)]
        rise = rise_ref[:, cols(h)]
        tail = tail_ref[:, cols(h)]
        bh = b[:, cols(h)]
        k_tail = k * tail
        q_gate = q * rise
        for n in range(blocks):
            width = (n + 1) * GROUP
            keys = [k_tail[rows(m), :] * jnp.exp(sum((c[j][:, cols(h)] for j in range(m + 1, n)),
                                                     jnp.zeros((1, K), F32)))
                    for m in range(n)]
            keys.append(k[rows(n), :] * jnp.exp(-bh[rows(n), :]))
            keys = split(jnp.concatenate(keys, axis=0))
            dots = mm_nt(do[rows(n), :], v[:width, :])
            t = lax.broadcasted_iota(jnp.int32, (GROUP, width), 0) + n * GROUP
            s = lax.broadcasted_iota(jnp.int32, (GROUP, width), 1)
            dots = split(jnp.where(s <= t, dots, 0.0))
            acc_q[rows(n), cols(h)] = rise[rows(n), :] * three(mm, dots, keys)

            length = L - n * GROUP
            tops = [q[rows(n), :] * jnp.exp(bh[rows(n), :] - c[n][:, cols(h)])]
            tops += [q_gate[rows(m), :] * jnp.exp(sum((c[j][:, cols(h)] for j in range(n + 1, m)),
                                                      jnp.zeros((1, K), F32)))
                     for m in range(n + 1, blocks)]
            tops = split(jnp.concatenate(tops, axis=0))
            s = lax.broadcasted_iota(jnp.int32, (GROUP, length), 0)
            t = lax.broadcasted_iota(jnp.int32, (GROUP, length), 1)
            causal = s <= t
            dots = mm_nt(v[rows(n), :], do[n * GROUP:, :])
            dots = split(jnp.where(causal, dots, 0.0))
            acc_k[rows(n), cols(h)] = tail[rows(n), :] * three(mm, dots, tops)
            scores = three(mm_nt, split(k_tail[rows(n), :]), tops)
            scores = split(jnp.where(causal, scores, 0.0))
            acc_v[rows(n), vcols(h)] = mm(scores[0], do[n * GROUP:, :]) + mm(scores[1], do[n * GROUP:, :])

    ec_copy.wait_recv()
    for i in range(chunks):
        h, r = part(i)
        px_copy(i).wait_recv()

        @pl.when(has_src)
        def _():
            far_copy(i).wait_recv()
            ent[mine, h, r] = px[h, r] + ec_par[h, 0:1, :] * carry[h, r]

        @pl.when(jnp.logical_not(has_src))
        def _():
            ent[mine, h, r] = px[h, r]

        @pl.when(has_dst)
        def _():
            total[h, r] = loc[mine, h, r] + ec_own[h, 0:1, :] * ent[mine, h, r]
            far_copy(i).start()
            near_copy(i).start()

    @pl.when(jnp.logical_not(has_dst))
    def _():
        ent[other] = jnp.zeros((H, V, K), F32)

    upper = jnp.where(row <= col, 1.0, 0.0).astype(BF16)
    stores = []
    for h in range(H):
        @pl.when(has_dst)
        def _():
            for i in range(h * per_head, (h + 1) * per_head):
                hh, r = part(i)
                send(total.at[hh, r], ent.at[other, hh, r], near_send.at[i], near_recv.at[i],
                     near).wait_recv()

        start = ent[0, h]
        end = ent[1, h]
        start2 = split(start)
        end2 = split(end)
        a = mm(do_ref[:, vcols(h)], jnp.concatenate(start2, axis=1))
        dq = acc_q[:, cols(h)] + whole_rise[:, cols(h)] * (a[:, :K] + a[:, K:])
        a = mm(v_ref[:, vcols(h)], jnp.concatenate(end2, axis=1))
        dk = acc_k[:, cols(h)] + whole_tail[:, cols(h)] * (a[:, :K] + a[:, K:])
        ke = (kt_ref[0, :, cols(h)], kt_ref[1, :, cols(h)])
        dv = acc_v[:, vcols(h)] + three(mm_nt, ke, end2)
        dq_ref[:, cols(h)] = dq.astype(BF16)
        dk_ref[:, cols(h)] = dk.astype(BF16)
        dv_ref[:, vcols(h)] = dv.astype(BF16)
        leave = ec_own[h, 0:1, :] * start + loc[0, h]
        later = jnp.sum(leave * end, axis=0, keepdims=True)
        terms = split(q_ref[:, cols(h)].astype(F32) * dq - k_ref[:, cols(h)].astype(F32) * dk)
        a = mm(upper, jnp.concatenate(terms, axis=1))
        gd_ref[:, cols(h)] = a[:, :K] + a[:, K:] + later
        for j, (src, dst, cc) in enumerate(((dq_ref, dq_hbm, cols(h)), (dk_ref, dk_hbm, cols(h)),
                                            (dv_ref, dv_hbm, vcols(h)), (gd_ref, gd_hbm, cols(h)))):
            copy = pltpu.make_async_copy(src.at[:, cc], dst.at[:, cc], out_sem.at[4 * h + j])
            copy.start()
            stores.append(copy)

    ec_copy.wait_send()
    for i in range(chunks):
        px_copy(i).wait_send()

    @pl.when(has_dst)
    def _():
        for i in range(chunks):
            far_copy(i).wait_send()
            near_copy(i).wait_send()

    for copy in stores:
        copy.wait()


def local(n_seq, queries, keys, values, log_decay, out_grad):
    L, HK = queries.shape
    HV = values.shape[1]
    K, V = HK // H, HV // H
    chunks = H * (V // ROWS)
    dma = pltpu.SemaphoreType.DMA
    any_spec = pl.BlockSpec(memory_space=pl.ANY)
    return pl.pallas_call(
        functools.partial(kernel, n_seq, L, K, V),
        out_shape=(
            jax.ShapeDtypeStruct((L, HK), BF16),
            jax.ShapeDtypeStruct((L, HK), BF16),
            jax.ShapeDtypeStruct((L, HV), BF16),
            jax.ShapeDtypeStruct((L, HK), F32),
        ),
        in_specs=[any_spec] * 5,
        out_specs=(any_spec,) * 4,
        scratch_shapes=[
            pltpu.VMEM((L, HK), BF16), pltpu.VMEM((L, HK), BF16), pltpu.VMEM((L, HV), BF16),
            pltpu.VMEM((L, HK), F32), pltpu.VMEM((L, HV), BF16),
            pltpu.VMEM((L, HK), BF16), pltpu.VMEM((L, HK), BF16), pltpu.VMEM((L, HV), BF16),
            pltpu.VMEM((L, HK), F32),
            pltpu.VMEM((L, HK), F32), pltpu.VMEM((L, HK), F32), pltpu.VMEM((L, HV), F32),
            pltpu.VMEM((L, HK), F32), pltpu.VMEM((L, HK), F32),
            pltpu.VMEM((L, HK), F32), pltpu.VMEM((L, HK), F32),
            pltpu.VMEM((2, L, HK), BF16), pltpu.VMEM((8, 128), F32),
            pltpu.VMEM((2, H, V, K), F32), pltpu.VMEM((H, V, K), F32), pltpu.VMEM((H, V, K), F32),
            pltpu.VMEM((H, V, K), F32), pltpu.VMEM((2, H, V, K), F32),
            pltpu.VMEM((H, 8, K), F32), pltpu.VMEM((H, 8, K), F32),
            dma((5,)), dma((8,)), dma((2,)), dma((chunks,)), dma((chunks,)), dma((chunks,)),
            dma((chunks,)), dma((chunks,)), dma((chunks,)),
        ],
        compiler_params=pltpu.CompilerParams(collective_id=0, has_side_effects=True),
    )(queries, keys, values, log_decay, out_grad)


def solution(mesh):
    n_seq = mesh.shape["seq"]
    spec = P(("batch", "seq"), None)
    return jax.shard_map(
        functools.partial(local, n_seq),
        mesh=mesh,
        in_specs=(spec,) * 5,
        out_specs=(spec,) * 4,
        check_vma=False,
    )
```

time: 154 us -> 34.3 us (0.22)
  waiting for transfers between devices: 48 us -> 0 us
  blocking collectives: 47.3 us -> 0 us
  Pallas kernels: 0 us -> 29.4 us
  other arithmetic: 23.3 us -> 0 us
  between operations: 14.3 us -> 0.66 us
  matrix products: 10.6 us -> 0 us
  local copies, waits for them, and re-layouts: 9.71 us -> 4.03 us
    all_gather x2 -> x0, waiting for transfers between devices: 47.3 us -> none  [carried_in(): gathered = jax.tree.map(lambda a: lax.all_gather(a, axis), part)]
    all_gather x2 -> x0, blocking collectives: 47.3 us -> none  [carried_in(): gathered = jax.tree.map(lambda a: lax.all_gather(a, axis), part)]
    pallas_call x0 -> x1, Pallas kernels: none -> 29.4 us  [local(): pl.pallas_call(functools.partial(kernel, n_seq, L, K, V), out_shape=(jax....]
    dot_general x10 -> x0, matrix products: 10.6 us -> none  [the longest x9 9.71 us: outer_product(): jnp.einsum(form, left, right, precision=HIGHEST_PRECISION, preferred_elem...]
    add x9 -> x0, other arithmetic: 9.29 us -> none  [the longest x4 4.28 us: backward_step(): start_grad + jnp.exp(summed_decay)[..., None] * carried_gradient]
    reduce_sum x8 -> x0, other arithmetic: 8.46 us -> none  [the longest x7 8.44 us: joined_combine(): jnp.sum(earlier[1] * later_one[2], axis=-1)]
    convert_element_type x6 -> x0, local copies, waits for them, and re-layouts: 3.35 us -> none  [the longest x1 1.03 us: local(): key_rows = keys.reshape(blocks, GROUP, H, K).astype(jnp.float32)]
    dynamic_update_slice x8 -> x0, other arithmetic: 2.98 us -> none  [local(): lax.scan(forward_step, zero_state, (block_sum, local_ends))]
  transfers between devices with their start and end apart: 2 -> 0, of which waited for: 2 -> 0; matrix products, arithmetic and copies ran while one was open for 4% -> 0% of each run, Pallas kernels for 0% -> 0%
where the time goes in v1:
time: 34.3 us; the launch traced here: 34.1 us
  Pallas kernels  29.4 us (86%)
  local copies, waits for them, and re-layouts  4.03 us (12%)
  between operations  0.66 us (2%)
    pallas_call x1, Pallas kernels, local(): pl.pallas_call(functools.partial(kernel, n_seq, L, K, V), out_shape=(jax....  29.4 us
    unnamed x10, local copies, waits for them, and re-layouts  4.03 us

profile of v1, /device:TPU:0, one launch (start us, length us, event | category | flops | bytes accessed | tf_op | source)
XLA Modules:
  0.0 34.1 jit_solution(16216734408497926901)
XLA Ops:
  0.6 29.4 %shard_map.84 = (bf16[256,256]{1,0:T(8,128)(2,1)}, bf16[256,256]{1,0:T(8,128)(2,1)}, bf16[256,512]{1,0:T(8,128)(2,1)}, f32[256,256]{1,0:T(8,128)}) custom-call(bf16[256,256]{1,0:T(8,128)(2,1)} %q_hbm.1, bf16[256,256]{1,0:T(8,128)(2,1)} %k_hbm.1, bf16[256,512]{1,0:T(8,128)(2,1)} %v_hbm.1, f32[256,256]{1,0:T(8,128)} %ld_hbm.1, bf16[256,512]{1,0:T(8,128)(2,1)} %do_hbm.1), custom_call_target="tpu_custom_call" | custom-call | tf_op jit(solution)/shard_map/pallas_call | solution.py:284
  30.0 0.0 copy-start.2
  30.0 0.0 copy-start.1
  30.0 1.6 %copy.13 = bf16[256,256]{1,0:T(8,128)(2,1)} copy(bf16[256,256]{1,0:T(8,128)(2,1)} %get-tuple-element.8) | data formatting | bytes 262144
  31.7 0.0 copy-done.2
  31.7 0.7 %copy.14 = bf16[256,256]{1,0:T(8,128)(2,1)} copy(bf16[256,256]{1,0:T(8,128)(2,1)S(1)} %copy-done.2) | data formatting | bytes 262144
  32.3 0.0 copy-done.1
  32.3 0.0 copy-start
  32.3 0.7 %copy.15 = bf16[256,512]{1,0:T(8,128)(2,1)} copy(bf16[256,512]{1,0:T(8,128)(2,1)S(1)} %copy-done.1) | data formatting | bytes 524288
  33.0 0.3 copy-done
  33.4 0.7 %copy.16 = f32[256,256]{1,0:T(8,128)} copy(f32[256,256]{1,0:T(8,128)S(1)} %copy-done) | data formatting | bytes 524288
Async XLA Ops:
  30.0 1.6 %copy-start.2 = (bf16[256,256]{1,0:T(8,128)(2,1)S(1)}, bf16[256,256]{1,0:T(8,128)(2,1)}, u32[]{:S(2)}) copy-start(bf16[256,256]{1,0:T(8,128)(2,1)} %get-tuple-element.9) | copy-start | bytes 393220
  30.0 2.3 %copy-start.1 = (bf16[256,512]{1,0:T(8,128)(2,1)S(1)}, bf16[256,512]{1,0:T(8,128)(2,1)}, u32[]{:S(2)}) copy-start(bf16[256,512]{1,0:T(8,128)(2,1)} %get-tuple-element.10) | copy-start | bytes 786436
  32.3 1.0 %copy-start = (f32[256,256]{1,0:T(8,128)S(1)}, f32[256,256]{1,0:T(8,128)}, u32[]{:S(2)}) copy-start(f32[256,256]{1,0:T(8,128)} %get-tuple-element.11) | copy-start | bytes 786436

commit v2 on v1

--- a/solution.py
+++ b/solution.py
@@ -38,12 +38,11 @@
 
 def kernel(n_seq, L, K, V,
            q_hbm, k_hbm, v_hbm, ld_hbm, do_hbm,
-           dq_hbm, dk_hbm, dv_hbm, gd_hbm,
+           dq_ref, dk_ref, dv_ref, gd_ref,
            q_ref, k_ref, v_ref, ld_ref, do_ref,
-           dq_ref, dk_ref, dv_ref, gd_ref,
-           acc_q, acc_k, acc_v, rise_ref, tail_ref, whole_rise, whole_tail, kt_ref, qg_ref,
+           acc_q, acc_k, acc_v, rise_ref, tail_ref, whole_rise, whole_tail, kt_ref,
            loc, px, carry, total, ent, ec_own, ec_par,
-           in_sem, out_sem, ec_sem, px_send, px_recv, near_send, near_recv, far_send, far_recv):
+           in_sem, ec_sem, px_send, px_recv, near_send, near_recv, far_send, far_recv):
     blocks = L // GROUP
     per_head = V // ROWS
     chunks = H * per_head
@@ -58,7 +57,7 @@
     back = me - 2 * sign
     has_dst = jnp.logical_and(far >= 0, far < n_seq)
     has_src = jnp.logical_and(back >= 0, back < n_seq)
-    peers = 1 + 2 * has_dst.astype(jnp.int32) + has_src.astype(jnp.int32)
+    peers = 1 + has_dst.astype(jnp.int32) + has_src.astype(jnp.int32)
     barrier = pltpu.get_barrier_semaphore()
 
     loads = [
@@ -78,7 +77,6 @@
 
     @pl.when(has_dst)
     def _():
-        tell(near)
         tell(far)
 
     @pl.when(has_src)
@@ -138,7 +136,7 @@
 
     def near_copy(i):
         h, r = part(i)
-        return send(total.at[h, r], ent.at[mine, h, r], near_send.at[i], near_recv.at[i], near)
+        return send(carry.at[h, r], ent.at[mine, h, r], near_send.at[i], near_recv.at[i], partner)
 
     def far_copy(i):
         h, r = part(i)
@@ -162,6 +160,19 @@
             ec_copy.start()
         for i in range(h * per_head, (h + 1) * per_head):
             px_copy(i).start()
+
+    @pl.when(jnp.logical_not(has_src))
+    def _():
+        ec_copy.wait_recv()
+        for i in range(chunks):
+            h, r = part(i)
+            px_copy(i).wait_recv()
+            ent[mine, h, r] = px[h, r]
+
+            @pl.when(has_dst)
+            def _():
+                total[h, r] = loc[mine, h, r] + ec_own[h, 0:1, :] * px[h, r]
+                far_copy(i).start()
 
     for h in range(H):
         k = k_ref[:, cols(h)].astype(F32)
@@ -202,39 +213,34 @@
             scores = split(jnp.where(causal, scores, 0.0))
             acc_v[rows(n), vcols(h)] = mm(scores[0], do[n * GROUP:, :]) + mm(scores[1], do[n * GROUP:, :])
 
-    ec_copy.wait_recv()
-    for i in range(chunks):
-        h, r = part(i)
-        px_copy(i).wait_recv()
-
-        @pl.when(has_src)
-        def _():
+    @pl.when(has_src)
+    def _():
+        ec_copy.wait_recv()
+        for i in range(chunks):
+            h, r = part(i)
+            px_copy(i).wait_recv()
             far_copy(i).wait_recv()
-            ent[mine, h, r] = px[h, r] + ec_par[h, 0:1, :] * carry[h, r]
-
-        @pl.when(jnp.logical_not(has_src))
-        def _():
-            ent[mine, h, r] = px[h, r]
-
-        @pl.when(has_dst)
-        def _():
-            total[h, r] = loc[mine, h, r] + ec_own[h, 0:1, :] * ent[mine, h, r]
-            far_copy(i).start()
             near_copy(i).start()
+            start = px[h, r] + ec_par[h, 0:1, :] * carry[h, r]
+            ent[mine, h, r] = start
+
+            @pl.when(has_dst)
+            def _():
+                total[h, r] = loc[mine, h, r] + ec_own[h, 0:1, :] * start
+                far_copy(i).start()
 
     @pl.when(jnp.logical_not(has_dst))
     def _():
         ent[other] = jnp.zeros((H, V, K), F32)
 
     upper = jnp.where(row <= col, 1.0, 0.0).astype(BF16)
-    stores = []
     for h in range(H):
         @pl.when(has_dst)
         def _():
             for i in range(h * per_head, (h + 1) * per_head):
                 hh, r = part(i)
-                send(total.at[hh, r], ent.at[other, hh, r], near_send.at[i], near_recv.at[i],
-                     near).wait_recv()
+                send(carry.at[hh, r], ent.at[other, hh, r], near_send.at[i], near_recv.at[i],
+                     partner).wait_recv()
 
         start = ent[0, h]
         end = ent[1, h]
@@ -254,11 +260,6 @@
         terms = split(q_ref[:, cols(h)].astype(F32) * dq - k_ref[:, cols(h)].astype(F32) * dk)
         a = mm(upper, jnp.concatenate(terms, axis=1))
         gd_ref[:, cols(h)] = a[:, :K] + a[:, K:] + later
-        for j, (src, dst, cc) in enumerate(((dq_ref, dq_hbm, cols(h)), (dk_ref, dk_hbm, cols(h)),
-                                            (dv_ref, dv_hbm, vcols(h)), (gd_ref, gd_hbm, cols(h)))):
-            copy = pltpu.make_async_copy(src.at[:, cc], dst.at[:, cc], out_sem.at[4 * h + j])
-            copy.start()
-            stores.append(copy)
 
     ec_copy.wait_send()
     for i in range(chunks):
@@ -268,9 +269,19 @@
     def _():
         for i in range(chunks):
             far_copy(i).wait_send()
+
+    @pl.when(has_src)
+    def _():
+        for i in range(chunks):
             near_copy(i).wait_send()
 
-    for copy in stores:
+
+def store_kernel(*refs):
+    sems = refs[8]
+    copies = [pltpu.make_async_copy(refs[i], refs[4 + i], sems.at[i]) for i in range(4)]
+    for copy in copies:
+        copy.start()
+    for copy in copies:
         copy.wait()
 
 
@@ -281,33 +292,35 @@
     chunks = H * (V // ROWS)
     dma = pltpu.SemaphoreType.DMA
     any_spec = pl.BlockSpec(memory_space=pl.ANY)
-    return pl.pallas_call(
+    shapes = (((L, HK), BF16), ((L, HK), BF16), ((L, HV), BF16), ((L, HK), F32))
+    held = pl.pallas_call(
         functools.partial(kernel, n_seq, L, K, V),
-        out_shape=(
-            jax.ShapeDtypeStruct((L, HK), BF16),
-            jax.ShapeDtypeStruct((L, HK), BF16),
-            jax.ShapeDtypeStruct((L, HV), BF16),
-            jax.ShapeDtypeStruct((L, HK), F32),
-        ),
+        out_shape=tuple(pltpu.VMEM(*a) for a in shapes),
         in_specs=[any_spec] * 5,
-        out_specs=(any_spec,) * 4,
+        out_specs=(pl.BlockSpec(memory_space=pltpu.VMEM),) * 4,
         scratch_shapes=[
             pltpu.VMEM((L, HK), BF16), pltpu.VMEM((L, HK), BF16), pltpu.VMEM((L, HV), BF16),
             pltpu.VMEM((L, HK), F32), pltpu.VMEM((L, HV), BF16),
-            pltpu.VMEM((L, HK), BF16), pltpu.VMEM((L, HK), BF16), pltpu.VMEM((L, HV), BF16),
-            pltpu.VMEM((L, HK), F32),
             pltpu.VMEM((L, HK), F32), pltpu.VMEM((L, HK), F32), pltpu.VMEM((L, HV), F32),
             pltpu.VMEM((L, HK), F32), pltpu.VMEM((L, HK), F32),
             pltpu.VMEM((L, HK), F32), pltpu.VMEM((L, HK), F32),
-            pltpu.VMEM((2, L, HK), BF16), pltpu.VMEM((8, 128), F32),
+            pltpu.VMEM((2, L, HK), BF16),
             pltpu.VMEM((2, H, V, K), F32), pltpu.VMEM((H, V, K), F32), pltpu.VMEM((H, V, K), F32),
             pltpu.VMEM((H, V, K), F32), pltpu.VMEM((2, H, V, K), F32),
             pltpu.VMEM((H, 8, K), F32), pltpu.VMEM((H, 8, K), F32),
-            dma((5,)), dma((8,)), dma((2,)), dma((chunks,)), dma((chunks,)), dma((chunks,)),
+            dma((5,)), dma((2,)), dma((chunks,)), dma((chunks,)), dma((chunks,)),
             dma((chunks,)), dma((chunks,)), dma((chunks,)),
         ],
         compiler_params=pltpu.CompilerParams(collective_id=0, has_side_effects=True),
     )(queries, keys, values, log_decay, out_grad)
+    return pl.pallas_call(
+        store_kernel,
+        out_shape=tuple(jax.ShapeDtypeStruct(*a) for a in shapes),
+        in_specs=[any_spec] * 4,
+        out_specs=(any_spec,) * 4,
+        scratch_shapes=[dma((4,))],
+        compiler_params=pltpu.CompilerParams(vmem_limit_bytes=1 << 20),
+    )(*held)
 
 
 def solution(mesh):

time: 34.3 us -> 25.3 us (0.74)
  Pallas kernels: 29.4 us -> 24.5 us
  local copies, waits for them, and re-layouts: 4.03 us -> 0 us
    pallas_call x1 -> x2, Pallas kernels: 29.4 us -> 24.5 us  [the longest x1 23.6 us: local(): pl.pallas_call(functools.partial(kernel, n_seq, L, K, V), out_shape=tuple...]
    unnamed x10 -> x0, local copies, waits for them, and re-layouts: 4.03 us -> none
where the time goes in v2:
time: 25.3 us; the launch traced here: 25.1 us
  Pallas kernels  24.5 us (97%)
  between operations  0.64 us (3%)
    pallas_call x1, Pallas kernels, local(): pl.pallas_call(functools.partial(kernel, n_seq, L, K, V), out_shape=tuple...  23.6 us
    pallas_call x1, Pallas kernels, local(): pl.pallas_call(store_kernel, out_shape=tuple((jax.ShapeDtypeStruct(*a) fo...  0.91 us

profile of v2, /device:TPU:0, one launch (start us, length us, event | category | flops | bytes accessed | tf_op | source)
XLA Modules:
  0.0 25.1 jit_solution(10551633640432628606)
XLA Ops:
  0.6 23.6 %shard_map.84 = (bf16[256,256]{1,0:T(8,128)(2,1)S(1)}, bf16[256,256]{1,0:T(8,128)(2,1)S(1)}, bf16[256,512]{1,0:T(8,128)(2,1)S(1)}, f32[256,256]{1,0:T(8,128)S(1)}) custom-call(bf16[256,256]{1,0:T(8,128)(2,1)} %q_hbm.1, bf16[256,256]{1,0:T(8,128)(2,1)} %k_hbm.1, bf16[256,512]{1,0:T(8,128)(2,1)} %v_hbm.1, f32[256,256]{1,0:T(8,128)} %ld_hbm.1, ...), custom_call_target="tpu_custom_call" | custom-call | tf_op jit(solution)/shard_map/pallas_call | solution.py:296
  24.2 0.9 %shard_map.85 = (bf16[256,256]{1,0:T(8,128)(2,1)}, bf16[256,256]{1,0:T(8,128)(2,1)}, bf16[256,512]{1,0:T(8,128)(2,1)}, f32[256,256]{1,0:T(8,128)}) custom-call(bf16[256,256]{1,0:T(8,128)(2,1)S(1)} %get-tuple-element.8.refs_0_, bf16[256,256]{1,0:T(8,128)(2,1)S(1)} %get-tuple-element.9.refs_1_, bf16[256,512]{1,0:T(8,128)(2,1)S(1)} %get-tuple-element.10.refs_2_, ...), custom_call_target="tpu_custom_call" | custom-call | tf_op jit(solution)/shard_map/pallas_call | solution.py:316

commit v3 on v2

v3 whole, which is shorter than its diff:
```python
import functools

import jax
import jax.numpy as jnp
from jax import lax
from jax.experimental import pallas as pl
from jax.experimental.pallas import tpu as pltpu
from jax.sharding import PartitionSpec as P

H = 2
GROUP = 64
ROWS = 32

F32 = jnp.float32
BF16 = jnp.bfloat16


def split(x):
    hi = x.astype(BF16)
    return hi, (x - hi.astype(F32)).astype(BF16)


def mm(a, b):
    return lax.dot_general(a, b, (((1,), (0,)), ((), ())), preferred_element_type=F32)


def mm_nt(a, b):
    return lax.dot_general(a, b, (((1,), (1,)), ((), ())), preferred_element_type=F32)


def mm_tn(a, b):
    return lax.dot_general(a, b, (((0,), (0,)), ((), ())), preferred_element_type=F32)


def three(dot, a, b):
    return dot(a[0], b[0]) + dot(a[0], b[1]) + dot(a[1], b[0])


def kernel(n_seq, L, K, V,
           q_hbm, k_hbm, v_hbm, ld_hbm, do_hbm,
           dq_ref, dk_ref, dv_ref, gd_ref,
           qk_ref, vd_ref, ld_ref,
           acc_q, acc_k, acc_v, rise_ref, tail_ref, whole,
           loc, px, carry, total, relay, ent, ec_own, ec_par,
           in_sem, ec_sem, px_send, px_recv, near_send, near_recv, far_send, far_recv):
    blocks = L // GROUP
    per_head = V // ROWS
    me = lax.axis_index("seq")
    odd = lax.rem(me, 2)
    late = (2 * me >= n_seq).astype(jnp.int32)
    partner = me + 1 - 2 * odd
    up = me + 2 < n_seq
    down = me - 2 >= 0
    sign = (2 * odd - 1, 1 - 2 * odd)
    first = lax.rem(odd + late, 2)
    barrier = pltpu.get_barrier_semaphore()

    def pick(h, x0, x1):
        return jnp.where(h == 0, x0, x1)

    def other_of(h):
        return pick(h, odd, 1 - odd)

    def sign_of(h):
        return pick(h, sign[0], sign[1])

    def reached(device):
        return jnp.logical_and(device >= 0, device < n_seq)

    def has_dst(h):
        return reached(me + 2 * sign_of(h))

    def has_src(h):
        return reached(me - 2 * sign_of(h))

    loads = [
        pltpu.make_async_copy(src, dst, in_sem.at[i])
        for i, (src, dst) in enumerate(
            ((ld_hbm, ld_ref), (k_hbm, qk_ref.at[0]), (q_hbm, qk_ref.at[1]),
             (v_hbm, vd_ref.at[0]), (do_hbm, vd_ref.at[1]))
        )
    ]
    for copy in loads:
        copy.start()

    def tell(device):
        pl.semaphore_signal(barrier, inc=1, device_id={"seq": device},
                            device_id_type=pl.DeviceIdType.MESH)

    tell(partner)

    @pl.when(up)
    def _():
        tell(me + 2)

    @pl.when(down)
    def _():
        tell(me - 2)

    loads[0].wait()
    row = lax.broadcasted_iota(jnp.int32, (L, L), 0)
    col = lax.broadcasted_iota(jnp.int32, (L, L), 1)
    within = jnp.logical_and(row >= col, row // GROUP == col // GROUP)
    tri = jnp.where(within, 1.0, 0.0).astype(BF16)
    ld = ld_ref[...]
    ld0, rest = split(ld)
    mid = ld - ld0.astype(F32)
    low = (mid - rest.astype(F32)).astype(BF16)
    b = mm(tri, ld0) + mm(tri, rest) + mm(tri, low)

    def rows(n):
        return slice(n * GROUP, (n + 1) * GROUP)

    def cols(h):
        return slice(h * K, (h + 1) * K)

    def vcols(h):
        return slice(h * V, (h + 1) * V)

    c = [b[(n + 1) * GROUP - 1:(n + 1) * GROUP, :] for n in range(blocks)]
    before = [jnp.zeros_like(c[0])]
    for n in range(blocks):
        before.append(before[-1] + c[n])
    after = [jnp.zeros_like(c[0])]
    for n in reversed(range(blocks)):
        after.insert(0, after[0] + c[n])
    for n in range(blocks):
        bn = b[rows(n), :]
        rise = jnp.exp(bn)
        tail = jnp.exp(c[n] - bn)
        rise_ref[rows(n), :] = rise
        tail_ref[rows(n), :] = tail
        whole[1, rows(n), :] = rise * jnp.exp(before[n])
        whole[0, rows(n), :] = tail * jnp.exp(after[n + 1])
    gone = jnp.exp(before[blocks])
    for h in range(H):
        ec_own[h] = jnp.broadcast_to(gone[:, cols(h)], (8, K))

    def send(src, dst, ssem, rsem, device):
        return pltpu.make_async_remote_copy(
            src_ref=src, dst_ref=dst, send_sem=ssem, recv_sem=rsem,
            device_id={"seq": device}, device_id_type=pl.DeviceIdType.MESH)

    def part(i):
        return pl.ds(i * ROWS, ROWS)

    def px_copy(h, i):
        r = part(i)
        return send(loc.at[other_of(h), h, r], px.at[h, r], px_send.at[h, i], px_recv.at[h, i], partner)

    def near_copy(h, i):
        r = part(i)
        return send(relay.at[h, r], ent.at[1 - other_of(h), h, r], near_send.at[h, i],
                    near_recv.at[h, i], partner)

    def far_copy(h, i):
        r = part(i)
        return send(total.at[h, r], carry.at[h, r], far_send.at[h, i], far_recv.at[h, i],
                    me + 2 * sign_of(h))

    ec_copy = send(ec_own, ec_par, ec_sem.at[0], ec_sem.at[1], partner)

    for copy in loads[1:]:
        copy.wait()

    def device_total(slot, h):
        kc = pl.ds(pl.multiple_of(h * K, K), K)
        vc = pl.ds(pl.multiple_of(h * V, V), V)
        x = split(qk_ref[slot, :, kc].astype(F32) * whole[slot, :, kc])
        e = mm_tn(vd_ref[slot, :, vc], jnp.concatenate(x, axis=1))
        loc[slot, h] = e[:, :K] + e[:, K:]

    device_total(other_of(first), first)
    pl.semaphore_wait(barrier, 1 + up.astype(jnp.int32) + down.astype(jnp.int32))
    for i in range(per_head):
        px_copy(first, i).start()
    ec_copy.start()
    device_total(other_of(1 - first), 1 - first)
    for i in range(per_head):
        px_copy(1 - first, i).start()
    device_total(1 - other_of(1 - first), 1 - first)
    device_total(1 - other_of(first), first)

    def chain(h, i):
        r = part(i)
        px_copy(h, i).wait_recv()

        @pl.when(has_src(h))
        def _():
            far_copy(h, i).wait_recv()

        mine = 1 - other_of(h)
        came = carry[h, r]
        got = px[h, r]
        own = loc[mine, h, r]

        @pl.when(h == 0)
        def _():
            middle = got + ec_par[h, 0:1, :] * came
            relay[h, r] = came
            ent[mine, h, r] = middle
            total[h, r] = own + ec_own[h, 0:1, :] * middle

        @pl.when(h != 0)
        def _():
            middle = own + ec_own[h, 0:1, :] * came
            relay[h, r] = middle
            ent[mine, h, r] = came
            total[h, r] = got + ec_par[h, 0:1, :] * middle

        @pl.when(has_dst(h))
        def _():
            far_copy(h, i).start()

        @pl.when(jnp.logical_or(h != 0, has_src(h)))
        def _():
            near_copy(h, i).start()

    lead = 1 - first
    for h in range(H):
        @pl.when(jnp.logical_not(has_src(h)))
        def _():
            carry[h] = jnp.zeros((V, K), F32)

    ec_copy.wait_recv()

    @pl.when(jnp.logical_not(has_src(lead)))
    def _():
        for i in range(per_head):
            chain(lead, i)

    for h in range(H):
        k = qk_ref[0, :, cols(h)].astype(F32)
        q = qk_ref[1, :, cols(h)].astype(F32)
        v = vd_ref[0, :, vcols(h)]
        do = vd_ref[1, :, vcols(h)]
        rise = rise_ref[:, cols(h)]
        tail = tail_ref[:, cols(h)]
        bh = b[:, cols(h)]
        k_tail = k * tail
        q_gate = q * rise
        for n in range(blocks):
            width = (n + 1) * GROUP
            keys = [k_tail[rows(m), :] * jnp.exp(sum((c[j][:, cols(h)] for j in range(m + 1, n)),
                                                     jnp.zeros((1, K), F32)))
                    for m in range(n)]
            keys.append(k[rows(n), :] * jnp.exp(-bh[rows(n), :]))
            keys = split(jnp.concatenate(keys, axis=0))
            dots = mm_nt(do[rows(n), :], v[:width, :])
            t = lax.broadcasted_iota(jnp.int32, (GROUP, width), 0) + n * GROUP
            s = lax.broadcasted_iota(jnp.int32, (GROUP, width), 1)
            dots = split(jnp.where(s <= t, dots, 0.0))
            acc_q[rows(n), cols(h)] = rise[rows(n), :] * three(mm, dots, keys)

            length = L - n * GROUP
            tops = [q[rows(n), :] * jnp.exp(bh[rows(n), :] - c[n][:, cols(h)])]
            tops += [q_gate[rows(m), :] * jnp.exp(sum((c[j][:, cols(h)] for j in range(n + 1, m)),
                                                      jnp.zeros((1, K), F32)))
                     for m in range(n + 1, blocks)]
            tops = split(jnp.concatenate(tops, axis=0))
            s = lax.broadcasted_iota(jnp.int32, (GROUP, length), 0)
            t = lax.broadcasted_iota(jnp.int32, (GROUP, length), 1)
            causal = s <= t
            dots = mm_nt(v[rows(n), :], do[n * GROUP:, :])
            dots = split(jnp.where(causal, dots, 0.0))
            acc_k[rows(n), cols(h)] = tail[rows(n), :] * three(mm, dots, tops)
            scores = three(mm_nt, split(k_tail[rows(n), :]), tops)
            scores = split(jnp.where(causal, scores, 0.0))
            acc_v[rows(n), vcols(h)] = mm(scores[0], do[n * GROUP:, :]) + mm(scores[1], do[n * GROUP:, :])

    lag = (5 * per_head) // 8
    for i in range(per_head + lag):
        if i < per_head:
            @pl.when(has_src(lead))
            def _():
                chain(lead, i)
        if i >= lag:
            chain(1 - lead, i - lag)

    @pl.when(jnp.logical_not(has_dst(0)))
    def _():
        ent[odd, 0] = jnp.zeros((V, K), F32)

    upper = jnp.where(row <= col, 1.0, 0.0).astype(BF16)
    for h in range(H):
        if h == 0:
            @pl.when(has_dst(0))
            def _():
                for i in range(per_head):
                    near_copy(0, i).wait_recv()
        else:
            for i in range(per_head):
                near_copy(h, i).wait_recv()

        start = ent[0, h]
        end = ent[1, h]
        start2 = split(start)
        end2 = split(end)
        a = mm(vd_ref[1, :, vcols(h)], jnp.concatenate(start2, axis=1))
        dq = acc_q[:, cols(h)] + whole[1, :, cols(h)] * (a[:, :K] + a[:, K:])
        a = mm(vd_ref[0, :, vcols(h)], jnp.concatenate(end2, axis=1))
        dk = acc_k[:, cols(h)] + whole[0, :, cols(h)] * (a[:, :K] + a[:, K:])
        ke = split(qk_ref[0, :, cols(h)].astype(F32) * whole[0, :, cols(h)])
        dv = acc_v[:, vcols(h)] + three(mm_nt, ke, end2)
        dq_ref[:, cols(h)] = dq.astype(BF16)
        dk_ref[:, cols(h)] = dk.astype(BF16)
        dv_ref[:, vcols(h)] = dv.astype(BF16)
        leave = ec_own[h, 0:1, :] * start + loc[0, h]
        later = jnp.sum(leave * end, axis=0, keepdims=True)
        terms = split(qk_ref[1, :, cols(h)].astype(F32) * dq - qk_ref[0, :, cols(h)].astype(F32) * dk)
        a = mm(upper, jnp.concatenate(terms, axis=1))
        gd_ref[:, cols(h)] = a[:, :K] + a[:, K:] + later

    ec_copy.wait_send()
    for h in range(H):
        for i in range(per_head):
            px_copy(h, i).wait_send()

        @pl.when(has_dst(h))
        def _():
            for i in range(per_head):
                far_copy(h, i).wait_send()

        if h == 0:
            @pl.when(has_src(0))
            def _():
                for i in range(per_head):
                    near_copy(0, i).wait_send()
        else:
            for i in range(per_head):
                near_copy(h, i).wait_send()


def store_kernel(*refs):
    sems = refs[8]
    copies = [pltpu.make_async_copy(refs[i], refs[4 + i], sems.at[i]) for i in range(4)]
    for copy in copies:
        copy.start()
    for copy in copies:
        copy.wait()


def local(n_seq, queries, keys, values, log_decay, out_grad):
    L, HK = queries.shape
    HV = values.shape[1]
    K, V = HK // H, HV // H
    chunks = V // ROWS
    dma = pltpu.SemaphoreType.DMA
    any_spec = pl.BlockSpec(memory_space=pl.ANY)
    shapes = (((L, HK), BF16), ((L, HK), BF16), ((L, HV), BF16), ((L, HK), F32))
    held = pl.pallas_call(
        functools.partial(kernel, n_seq, L, K, V),
        out_shape=tuple(pltpu.VMEM(*a) for a in shapes),
        in_specs=[any_spec] * 5,
        out_specs=(pl.BlockSpec(memory_space=pltpu.VMEM),) * 4,
        scratch_shapes=[
            pltpu.VMEM((2, L, HK), BF16), pltpu.VMEM((2, L, HV), BF16), pltpu.VMEM((L, HK), F32),
            pltpu.VMEM((L, HK), F32), pltpu.VMEM((L, HK), F32), pltpu.VMEM((L, HV), F32),
            pltpu.VMEM((L, HK), F32), pltpu.VMEM((L, HK), F32), pltpu.VMEM((2, L, HK), F32),
            pltpu.VMEM((2, H, V, K), F32), pltpu.VMEM((H, V, K), F32), pltpu.VMEM((H, V, K), F32),
            pltpu.VMEM((H, V, K), F32), pltpu.VMEM((H, V, K), F32), pltpu.VMEM((2, H, V, K), F32),
            pltpu.VMEM((H, 8, K), F32), pltpu.VMEM((H, 8, K), F32),
            dma((5,)), dma((2,)), dma((H, chunks)), dma((H, chunks)), dma((H, chunks)),
            dma((H, chunks)), dma((H, chunks)), dma((H, chunks)),
        ],
        compiler_params=pltpu.CompilerParams(collective_id=0, has_side_effects=True),
    )(queries, keys, values, log_decay, out_grad)
    return pl.pallas_call(
        store_kernel,
        out_shape=tuple(jax.ShapeDtypeStruct(*a) for a in shapes),
        in_specs=[any_spec] * 4,
        out_specs=(any_spec,) * 4,
        scratch_shapes=[dma((4,))],
        compiler_params=pltpu.CompilerParams(vmem_limit_bytes=1 << 20),
    )(*held)


def solution(mesh):
    n_seq = mesh.shape["seq"]
    spec = P(("batch", "seq"), None)
    return jax.shard_map(
        functools.partial(local, n_seq),
        mesh=mesh,
        in_specs=(spec,) * 5,
        out_specs=(spec,) * 4,
        check_vma=False,
    )
```

time: 25.3 us -> 27.4 us (1.083)
  Pallas kernels: 24.5 us -> 26.7 us
    pallas_call x1, Pallas kernels: 23.6 us -> 25.7 us  [local(): pl.pallas_call(functools.partial(kernel, n_seq, L, K, V), out_shape=tuple...]
where the time goes in v3:
time: 27.4 us; the launch traced here: 27.3 us
  Pallas kernels  26.7 us (97%)
  between operations  0.64 us (2%)
    pallas_call x1, Pallas kernels, local(): pl.pallas_call(functools.partial(kernel, n_seq, L, K, V), out_shape=tuple...  25.7 us
    pallas_call x1, Pallas kernels, local(): pl.pallas_call(store_kernel, out_shape=tuple((jax.ShapeDtypeStruct(*a) fo...  0.91 us

profile of v3, /device:TPU:0, one launch (start us, length us, event | category | flops | bytes accessed | tf_op | source)
XLA Modules:
  0.0 27.3 jit_solution(10412599027456525982)
XLA Ops:
  0.6 25.7 %shard_map.84 = (bf16[256,256]{1,0:T(8,128)(2,1)S(1)}, bf16[256,256]{1,0:T(8,128)(2,1)S(1)}, bf16[256,512]{1,0:T(8,128)(2,1)S(1)}, f32[256,256]{1,0:T(8,128)S(1)}) custom-call(bf16[256,256]{1,0:T(8,128)(2,1)} %q_hbm.1, bf16[256,256]{1,0:T(8,128)(2,1)} %k_hbm.1, bf16[256,512]{1,0:T(8,128)(2,1)} %v_hbm.1, f32[256,256]{1,0:T(8,128)} %ld_hbm.1, ...), custom_call_target="tpu_custom_call" | custom-call | tf_op jit(solution)/shard_map/pallas_call | solution.py:351
  26.4 0.9 %shard_map.85 = (bf16[256,256]{1,0:T(8,128)(2,1)}, bf16[256,256]{1,0:T(8,128)(2,1)}, bf16[256,512]{1,0:T(8,128)(2,1)}, f32[256,256]{1,0:T(8,128)}) custom-call(bf16[256,256]{1,0:T(8,128)(2,1)S(1)} %get-tuple-element.8.refs_0_, bf16[256,256]{1,0:T(8,128)(2,1)S(1)} %get-tuple-element.9.refs_1_, bf16[256,512]{1,0:T(8,128)(2,1)S(1)} %get-tuple-element.10.refs_2_, ...), custom_call_target="tpu_custom_call" | custom-call | tf_op jit(solution)/shard_map/pallas_call | solution.py:368

commit v4 on v3

--- a/solution.py
+++ b/solution.py
@@ -9,7 +9,7 @@
 
 H = 2
 GROUP = 64
-ROWS = 32
+ROWS = 64
 
 F32 = jnp.float32
 BF16 = jnp.bfloat16
@@ -172,9 +172,9 @@
 
     device_total(other_of(first), first)
     pl.semaphore_wait(barrier, 1 + up.astype(jnp.int32) + down.astype(jnp.int32))
+    ec_copy.start()
     for i in range(per_head):
         px_copy(first, i).start()
-    ec_copy.start()
     device_total(other_of(1 - first), 1 - first)
     for i in range(per_head):
         px_copy(1 - first, i).start()
@@ -222,10 +222,9 @@
         def _():
             carry[h] = jnp.zeros((V, K), F32)
 
-    ec_copy.wait_recv()
-
     @pl.when(jnp.logical_not(has_src(lead)))
     def _():
+        ec_copy.wait_recv()
         for i in range(per_head):
             chain(lead, i)
 
@@ -267,6 +266,10 @@
             scores = three(mm_nt, split(k_tail[rows(n), :]), tops)
             scores = split(jnp.where(causal, scores, 0.0))
             acc_v[rows(n), vcols(h)] = mm(scores[0], do[n * GROUP:, :]) + mm(scores[1], do[n * GROUP:, :])
+
+    @pl.when(has_src(lead))
+    def _():
+        ec_copy.wait_recv()
 
     lag = (5 * per_head) // 8
     for i in range(per_head + lag):

time: 27.4 us -> 24.6 us (0.90)
  Pallas kernels: 26.7 us -> 23.8 us
    pallas_call x1, Pallas kernels: 25.7 us -> 22.9 us  [local(): pl.pallas_call(functools.partial(kernel, n_seq, L, K, V), out_shape=tuple...]
where the time goes in v4:
time: 24.6 us; the launch traced here: 24.5 us
  Pallas kernels  23.8 us (97%)
  between operations  0.64 us (3%)
    pallas_call x1, Pallas kernels, local(): pl.pallas_call(functools.partial(kernel, n_seq, L, K, V), out_shape=tuple...  22.9 us
    pallas_call x1, Pallas kernels, local(): pl.pallas_call(store_kernel, out_shape=tuple((jax.ShapeDtypeStruct(*a) fo...  0.91 us

profile of v4, /device:TPU:0, one launch (start us, length us, event | category | flops | bytes accessed | tf_op | source)
XLA Modules:
  0.0 24.5 jit_solution(3133124822820532994)
XLA Ops:
  0.6 22.9 %shard_map.84 = (bf16[256,256]{1,0:T(8,128)(2,1)S(1)}, bf16[256,256]{1,0:T(8,128)(2,1)S(1)}, bf16[256,512]{1,0:T(8,128)(2,1)S(1)}, f32[256,256]{1,0:T(8,128)S(1)}) custom-call(bf16[256,256]{1,0:T(8,128)(2,1)} %q_hbm.1, bf16[256,256]{1,0:T(8,128)(2,1)} %k_hbm.1, bf16[256,512]{1,0:T(8,128)(2,1)} %v_hbm.1, f32[256,256]{1,0:T(8,128)} %ld_hbm.1, ...), custom_call_target="tpu_custom_call" | custom-call | tf_op jit(solution)/shard_map/pallas_call | solution.py:354
  23.6 0.9 %shard_map.85 = (bf16[256,256]{1,0:T(8,128)(2,1)}, bf16[256,256]{1,0:T(8,128)(2,1)}, bf16[256,512]{1,0:T(8,128)(2,1)}, f32[256,256]{1,0:T(8,128)}) custom-call(bf16[256,256]{1,0:T(8,128)(2,1)S(1)} %get-tuple-element.8.refs_0_, bf16[256,256]{1,0:T(8,128)(2,1)S(1)} %get-tuple-element.9.refs_1_, bf16[256,512]{1,0:T(8,128)(2,1)S(1)} %get-tuple-element.10.refs_2_, ...), custom_call_target="tpu_custom_call" | custom-call | tf_op jit(solution)/shard_map/pallas_call | solution.py:371

commit v5 on v4

--- a/solution.py
+++ b/solution.py
@@ -97,11 +97,11 @@
     def _():
         tell(me - 2)
 
-    loads[0].wait()
     row = lax.broadcasted_iota(jnp.int32, (L, L), 0)
     col = lax.broadcasted_iota(jnp.int32, (L, L), 1)
     within = jnp.logical_and(row >= col, row // GROUP == col // GROUP)
     tri = jnp.where(within, 1.0, 0.0).astype(BF16)
+    loads[0].wait()
     ld = ld_ref[...]
     ld0, rest = split(ld)
     mid = ld - ld0.astype(F32)
@@ -194,26 +194,28 @@
         got = px[h, r]
         own = loc[mine, h, r]
 
+        def step(static, x1, e1, x2, e2):
+            middle = x1 + e1 * came
+            total[h, r] = x2 + e2 * middle
+
+            @pl.when(has_dst(h))
+            def _():
+                far_copy(h, i).start()
+
+            relay[h, r] = middle if static else came
+            ent[mine, h, r] = came if static else middle
+
         @pl.when(h == 0)
         def _():
-            middle = got + ec_par[h, 0:1, :] * came
-            relay[h, r] = came
-            ent[mine, h, r] = middle
-            total[h, r] = own + ec_own[h, 0:1, :] * middle
+            step(0, got, ec_par[h, 0:1, :], own, ec_own[h, 0:1, :])
+
+            @pl.when(has_src(h))
+            def _():
+                near_copy(h, i).start()
 
         @pl.when(h != 0)
         def _():
-            middle = own + ec_own[h, 0:1, :] * came
-            relay[h, r] = middle
-            ent[mine, h, r] = came
-            total[h, r] = got + ec_par[h, 0:1, :] * middle
-
-        @pl.when(has_dst(h))
-        def _():
-            far_copy(h, i).start()
-
-        @pl.when(jnp.logical_or(h != 0, has_src(h)))
-        def _():
+            step(1, own, ec_own[h, 0:1, :], got, ec_par[h, 0:1, :])
             near_copy(h, i).start()
 
     lead = 1 - first
@@ -271,7 +273,7 @@
     def _():
         ec_copy.wait_recv()
 
-    lag = (5 * per_head) // 8
+    lag = 3
     for i in range(per_head + lag):
         if i < per_head:
             @pl.when(has_src(lead))

time: 24.6 us -> 24.6 us (level)
  no operation moved by 1% of the time
where the time goes in v5:
time: 24.6 us; the launch traced here: 24.5 us
  Pallas kernels  23.8 us (97%)
  between operations  0.64 us (3%)
    pallas_call x1, Pallas kernels, local(): pl.pallas_call(functools.partial(kernel, n_seq, L, K, V), out_shape=tuple...  22.9 us
    pallas_call x1, Pallas kernels, local(): pl.pallas_call(store_kernel, out_shape=tuple((jax.ShapeDtypeStruct(*a) fo...  0.91 us

profile of v5, /device:TPU:0, one launch (start us, length us, event | category | flops | bytes accessed | tf_op | source)
XLA Modules:
  0.0 24.5 jit_solution(8433071618870994861)
XLA Ops:
  0.6 22.9 %shard_map.84 = (bf16[256,256]{1,0:T(8,128)(2,1)S(1)}, bf16[256,256]{1,0:T(8,128)(2,1)S(1)}, bf16[256,512]{1,0:T(8,128)(2,1)S(1)}, f32[256,256]{1,0:T(8,128)S(1)}) custom-call(bf16[256,256]{1,0:T(8,128)(2,1)} %q_hbm.1, bf16[256,256]{1,0:T(8,128)(2,1)} %k_hbm.1, bf16[256,512]{1,0:T(8,128)(2,1)} %v_hbm.1, f32[256,256]{1,0:T(8,128)} %ld_hbm.1, ...), custom_call_target="tpu_custom_call" | custom-call | tf_op jit(solution)/shard_map/pallas_call | solution.py:356
  23.6 0.9 %shard_map.85 = (bf16[256,256]{1,0:T(8,128)(2,1)}, bf16[256,256]{1,0:T(8,128)(2,1)}, bf16[256,512]{1,0:T(8,128)(2,1)}, f32[256,256]{1,0:T(8,128)}) custom-call(bf16[256,256]{1,0:T(8,128)(2,1)S(1)} %get-tuple-element.8.refs_0_, bf16[256,256]{1,0:T(8,128)(2,1)S(1)} %get-tuple-element.9.refs_1_, bf16[256,512]{1,0:T(8,128)(2,1)S(1)} %get-tuple-element.10.refs_2_, ...), custom_call_target="tpu_custom_call" | custom-call | tf_op jit(solution)/shard_map/pallas_call | solution.py:373
